TPU v7x, 512 devices: a whole 4x8x8 slice. The times are simulated.
512 devices in a mesh: seq: 64 (over z, x, core), head: 8 (over y).
Axes of the slice: x: 4, y: 8, z: 8, core: 2. Of those that a mesh axis runs over, the one named last changes fastest.
Arguments:
- queries: bfloat16 [65536, 3072], P('seq', 'head'), may hold values from -6 to 6
- keys: bfloat16 [65536, 3072], P('seq', 'head'), may hold values from -6 to 6
- values: bfloat16 [65536, 3072], P('seq', 'head'), may hold values from -6 to 6
- tile_pool: int32 [24, 1024], P('head'), may hold values from 0 to 511, as said below
- tile_lists: int32 [24, 512, 12], P('head', 'seq'), may hold values from 0 to 15, as said below
- key_slot: int32 [512], replicated, may hold values from 0 to 511, as said below
Outputs:
- attended: bfloat16 [65536, 3072], P(('seq', 'head'))
Inputs may be any that keep to these rules, and one draw needn't show every extreme that they name: `tile_pool`: for each index i of seq and each group of 3 heads (heads g * 3 onward), the pool entries of those heads for index i (columns i * 16 onward) name tiles whose slots lie on any one index of seq (slot // 8) at most 1 times, and exactly 1 times on some index. `tile_lists`: the 12 entries of one head and one query tile are distinct. `key_slot`: A permutation of the tiles that keeps tiles 0 to 3 at their own slots.
All inputs are finite; a program needn't handle non-finite values.
Results may differ from a plain program's by a relative error of at most 0.0043.
Values may be sent and summed in bfloat16 or wider, within the bound.
A program may use at most 64 MiB of HBM per device.

v0:
```python
import jax
import jax.numpy as jnp
from jax import lax
from jax.sharding import PartitionSpec as P

TILE = 128
SHARED = 4


def from_root(value, axis, source):
    kept = jnp.where(lax.axis_index(axis) == source, value, 0).astype(value.dtype)
    return lax.psum(kept, axis)


def arrange(matrix, tile_count, head_count, head_size):
    return matrix.reshape(tile_count, TILE, head_count, head_size).transpose(2, 0, 1, 3)


def finish(scores, value_part, pattern):
    tile_top = jnp.max(scores, -1)
    weights = jnp.exp(scores - tile_top[..., None])
    row_total = jnp.sum(weights, -1)
    numerator = jnp.einsum(
        pattern, weights.astype(jnp.bfloat16), value_part, preferred_element_type=jnp.float32
    )
    return (numerator, tile_top, row_total)


def blend_tiles(numerator, tile_top, row_total):
    overall = jnp.max(tile_top, 1, keepdims=True)
    factor = jnp.exp(tile_top - overall)
    upper = jnp.sum(factor[..., None] * numerator, 1)
    lower = jnp.sum(factor * row_total, 1)
    return (upper / lower[..., None]).astype(jnp.bfloat16)


def body(queries, keys, values, tile_pool, tile_lists, key_slot):
    seq_count = lax.axis_size("seq")
    my_index = lax.axis_index("seq")
    head_count, pool_total = tile_pool.shape
    pool_len = pool_total // seq_count
    list_len = tile_lists.shape[2]
    rows, width = queries.shape
    head_size = width // head_count
    tile_count = rows // TILE
    bound_slots = (head_count * pool_len + seq_count - 1) // seq_count
    block_tiles = min(tile_count, max(1, 512 // TILE))
    block_count = tile_count // block_tiles
    scaling = head_size ** (-0.5)
    query_heads = arrange(queries, tile_count, head_count, head_size)
    key_value = jnp.concatenate(
        [
            arrange(keys, tile_count, head_count, head_size),
            arrange(values, tile_count, head_count, head_size),
        ],
        -1,
    )
    flat_kv = key_value.reshape(head_count * tile_count, TILE, 2 * head_size)
    shared = from_root(key_value[:, :SHARED], "seq", 0)
    own_pool = lax.dynamic_slice_in_dim(tile_pool, my_index * pool_len, pool_len, 1)
    storage = key_slot[own_pool]
    owner_dev = (storage // tile_count).reshape(-1)
    head_ids = jnp.arange(head_count, dtype=jnp.int32)[:, None]
    req_code = (head_ids * tile_count + storage % tile_count).reshape(-1)
    matches = (owner_dev[:, None] == jnp.arange(seq_count, dtype=jnp.int32)[None, :]).astype(
        jnp.int32
    )
    slot_pos = jnp.sum((jnp.cumsum(matches, 0) - matches) * matches, 1)
    owner_dev, slot_pos, req_code = (owner_dev, slot_pos, req_code)
    outgoing = jnp.zeros((seq_count, bound_slots), jnp.int32).at[owner_dev, slot_pos].set(req_code)
    incoming = lax.all_to_all(outgoing, "seq", split_axis=0, concat_axis=0, tiled=True)
    replies = lax.all_to_all(flat_kv[incoming], "seq", split_axis=0, concat_axis=0, tiled=True)
    pool_tiles = replies[
        owner_dev.reshape(head_count, pool_len), slot_pos.reshape(head_count, pool_len)
    ]
    query_blocks = query_heads.reshape(head_count * block_count, block_tiles, TILE, head_size)
    list_blocks = tile_lists.reshape(head_count * block_count, block_tiles, list_len)
    head_of = jnp.arange(head_count * block_count, dtype=jnp.int32) // block_count

    def per_block(member):
        query_blk, list_blk, head_id = member
        listed = pool_tiles[head_id][list_blk]
        shared_head = shared[head_id]
        common = jnp.broadcast_to(shared_head[None], (block_tiles,) + shared_head.shape)
        keyset = jnp.concatenate([common, listed], 1)
        scores = (
            jnp.einsum(
                "tqd,tjkd->tjqk",
                query_blk,
                keyset[..., :head_size],
                preferred_element_type=jnp.float32,
            )
            * scaling
        )
        numerator, tile_top, row_total = finish(scores, keyset[..., head_size:], "tjqk,tjkd->tjqd")
        return blend_tiles(numerator, tile_top, row_total)

    per_blocks = lax.map(per_block, (query_blocks, list_blocks, head_of))
    per_heads = per_blocks.reshape(head_count, tile_count, TILE, head_size)
    result = per_heads.transpose(1, 2, 0, 3).reshape(rows, width)
    return lax.all_to_all(result, "head", split_axis=0, concat_axis=1, tiled=True)


def solution(mesh):
    return jax.shard_map(
        body,
        mesh=mesh,
        in_specs=(
            P("seq", "head"),
            P("seq", "head"),
            P("seq", "head"),
            P("head", None),
            P("head", "seq", None),
            P(),
        ),
        out_specs=P(("seq", "head"), None),
        check_vma=False,
    )
```

profile of v0, /device:TPU:1, one launch (start us, length us, event | category | flops | bytes accessed | tf_op | source)
XLA Modules:
  0.0 388.4 jit_solution(4417109201509644880)
XLA Ops:
  10.2 14.8 %all-to-all-start = ((s32[64,1,1]{2,1,0:T(1,128)}), s32[64,1,1]{2,1,0:T(1,128)S(1)}, u32[]{:S(2)}, u32[]{:S(2)}) async-start(s32[64,1,1]{2,1,0:T(1,128)} %copy.50), calls=%async_computation | async-start | bytes 65536 | tf_op jit(solution)/shard_map/all_to_all | solution.py:71
  25.1 1.4 copy.47
  27.2 1.3 pad_maximum_fusion.2
  28.5 2.2 copy.49
  30.6 3.8 all-to-all-done
  34.4 1.2 fusion.20
  35.6 2.8 gather_fusion.2
  38.4 6.9 %all-to-all-start.1 = ((bf16[64,1,128,256]{3,2,1,0:T(8,128)(2,1)}), bf16[64,1,128,256]{3,2,1,0:T(8,128)(2,1)}, u32[]{:S(2)}, u32[]{:S(2)}) async-start(bf16[64,1,128,256]{3,2,1,0:T(8,128)(2,1)} %bitcast.115), calls=%async_computation.1 | async-start | bytes 8388608 | tf_op jit(solution)/shard_map/all_to_all | solution.py:72
  45.3 1.3 fusion.19
  47.9 94.4 %all-to-all-done.1 = bf16[64,1,128,256]{3,2,1,0:T(8,128)(2,1)} async-done(((bf16[64,1,128,256]{3,2,1,0:T(8,128)(2,1)}), bf16[64,1,128,256]{3,2,1,0:T(8,128)(2,1)}, u32[]{:S(2)}, u32[]{:S(2)}) %all-to-all-start.1) | async-done | bytes 4194336 | tf_op jit(solution)/shard_map/all_to_all | solution.py:72
  142.3 4.7 %gather_fusion.3 = bf16[48,128,256]{2,1,0:T(8,128)(2,1)} fusion(bf16[64,1,128,256]{3,2,1,0:T(8,128)(2,1)} %all-to-all-done.1, s32[48]{0:T(128)S(1)} %reshape.314), kind=kCustom, calls=%fused_computation.3 | custom fusion | bytes 6291840 | tf_op jit(solution)/shard_map/gather | solution.py:73
  147.0 116.2 %all-reduce.2.cloned.1.call-done = bf16[3,4,128,256]{2,1,3,0:T(4,128)(2,1)} async-done(((bf16[3,4,128,256]{2,1,3,0:T(4,128)(2,1)}), bf16[3,4,128,256]{2,1,3,0:T(4,128)(2,1)}) %all-reduce.2.cloned.1.call-update) | async-done | bytes 786448 | tf_op jit(solution)/shard_map/psum | solution.py:12
  263.2 89.6 %while.10 = (s32[]{:T(128)}, bf16[6,4,128,128]{3,2,1,0:T(8,128)(2,1)S(1)}, s32[6]{0:T(128)S(1)}, bf16[3,4,128,256]{2,1,3,0:T(4,128)(2,1)}, bf16[3,16,128,256]{3,...) while((s32[]{:T(128)}, ...), condition=%wide.region_10.11_spmd, body=%wide.region_4.10_spmd.sunk | while | flops 553721984 | bytes 45364548 | solution.py:98
  265.7 1.3 dynamic-slice_bitcast_fusion.2
  267.8 2.5 gather_fusion
  270.3 1.0 constant_dynamic-slice_fusion.2
  271.7 2.1 bitcast_reduce_fusion.3
  273.8 1.3 fusion.37
  275.7 2.2 multiply_reduce_fusion.5
  280.7 1.3 dynamic-slice_bitcast_fusion.2
  282.8 2.5 gather_fusion
  285.3 1.0 constant_dynamic-slice_fusion.2
  286.6 2.1 bitcast_reduce_fusion.3
  288.8 1.3 fusion.37
  290.7 2.2 multiply_reduce_fusion.5
  295.6 1.3 dynamic-slice_bitcast_fusion.2
  297.7 2.5 gather_fusion
  301.6 2.1 bitcast_reduce_fusion.3
  303.7 1.3 fusion.37
  305.6 2.2 multiply_reduce_fusion.5
  310.6 1.3 dynamic-slice_bitcast_fusion.2
  312.6 2.5 gather_fusion
  315.2 1.0 constant_dynamic-slice_fusion.2
  316.5 2.1 bitcast_reduce_fusion.3
  318.7 1.3 fusion.37
  320.5 2.2 multiply_reduce_fusion.5
  325.5 1.3 dynamic-slice_bitcast_fusion.2
  327.6 2.5 gather_fusion
  331.4 2.1 bitcast_reduce_fusion.3
  333.6 1.3 fusion.37
  335.5 2.2 multiply_reduce_fusion.5
  340.5 1.3 dynamic-slice_bitcast_fusion.2
  342.5 2.5 gather_fusion
  346.4 2.1 bitcast_reduce_fusion.3
  348.6 1.3 fusion.37
  350.4 2.2 multiply_reduce_fusion.5
  353.7 26.3 %all_to_all.33 = bf16[8,128,384]{2,1,0:T(8,128)(2,1)S(1)} all-to-all(bf16[8,128,384]{2,1,0:T(8,128)(2,1)S(1)} %copy.56), channel_id=1, replica_groups=mesh['seq'=64,'head'=8] {'head'}, dimensions={0} | all-to-all | bytes 1572864 | tf_op jit(solution)/shard_map/all_to_all | solution.py:101
  380.3 1.2 copy.58
  (101 shorter events, 24.4 us)
Async XLA Ops:
  6.5 1.1 copy-start
  6.5 20.1 %copy-start.2 = (bf16[1024,384]{1,0:T(8,128)(2,1)S(1)}, bf16[1024,384]{1,0:T(8,128)(2,1)}, u32[]{:S(2)}) copy-start(bf16[1024,384]{1,0:T(8,128)(2,1)} %param.10) | copy-start | bytes 2359300
  10.2 24.1 %all-to-all-start = ((s32[64,1,1]{2,1,0:T(1,128)}), s32[64,1,1]{2,1,0:T(1,128)S(1)}, u32[]{:S(2)}, u32[]{:S(2)}) async-start(s32[64,1,1]{2,1,0:T(1,128)} %copy.50), calls=%async_computation | async-start | bytes 65536 | tf_op jit(solution)/shard_map/all_to_all | solution.py:71
  38.4 8.5 %copy-start.3 = (bf16[1024,384]{1,0:T(8,128)(2,1)S(1)}, bf16[1024,384]{1,0:T(8,128)(2,1)}, u32[]{:S(2)}) copy-start(bf16[1024,384]{1,0:T(8,128)(2,1)} %param.8) | copy-start | bytes 2359300
  38.4 103.9 %all-to-all-start.1 = ((bf16[64,1,128,256]{3,2,1,0:T(8,128)(2,1)}), bf16[64,1,128,256]{3,2,1,0:T(8,128)(2,1)}, u32[]{:S(2)}, u32[]{:S(2)}) async-start(bf16[64,1,128,256]{3,2,1,0:T(8,128)(2,1)} %bitcast.115), calls=%async_computation.1 | async-start | bytes 8388608 | tf_op jit(solution)/shard_map/all_to_all | solution.py:72
  45.3 217.9 %all-reduce.2.cloned.1.call-start = ((), (), s32[]{:S(2)}) async-start(), calls=%async_computation.3 | async-start | bytes 1572864 | tf_op jit(solution)/shard_map/psum | solution.py:12
  273.8 1.9 copy-start.1
  288.8 1.9 copy-start.1
  303.7 1.9 copy-start.1
  318.7 1.9 copy-start.1
  333.6 1.9 copy-start.1
  348.5 1.9 copy-start.1
Sparse Core Ops, SparseCore 0:
  49.6 213.6 all-reduce.1
where the time goes:
time: 392 us; the launch traced here: 388 us
  waiting for transfers between devices  214 us (55%)
  local copies, waits for them, and re-layouts  55.9 us (14%)
  matrix products  26.3 us (7%)
  blocking collectives  26.3 us (7%)
  starting transfers between devices  21.7 us (6%)
  other arithmetic  18.2 us (5%)
  between operations  13.6 us (3%)
  loops' own time  12.1 us (3%)
    psum x1, waiting for transfers between devices, from_root(): return lax.psum(kept, axis)  116 us
    all_to_all x1, waiting for transfers between devices, body(): lax.all_to_all(flat_kv[incoming], 'seq', split_axis=0, concat_axis=0, til...  94.4 us
    all_to_all x1, blocking collectives, body(): lax.all_to_all(result, 'head', split_axis=0, concat_axis=1, tiled=True)  26.3 us
    gather x6, local copies, waits for them, and re-layouts, per_block(): listed = pool_tiles[head_id][list_blk]  15.1 us
    all_to_all x1, starting transfers between devices, body(): lax.all_to_all(outgoing, 'seq', split_axis=0, concat_axis=0, tiled=True)  14.8 us
    dot_general x6, matrix products, finish(): jnp.einsum(pattern, weights.astype(jnp.bfloat16), value_part, preferred_e...  13.4 us
    dot_general x6, matrix products, per_block(): jnp.einsum('tqd,tjkd->tjqk', query_blk, keyset[..., :head_size], preferre...  12.9 us
    another operation x1, loops' own time, body(): per_blocks = lax.map(per_block, (query_blocks, list_blocks, head_of))  12.1 us
  transfers between devices with their start and end apart: 3, of which 3 were waited for; matrix products, arithmetic and copies ran while one was open for 3% of the time, Pallas kernels for 0%

commit v1 on v0

v1 whole, which is shorter than its diff:
```python
import functools
import math

import jax
import jax.numpy as jnp
from jax import lax
from jax.experimental import pallas as pl
from jax.experimental.pallas import tpu as pltpu
from jax.sharding import PartitionSpec as P

TILE = 128
HD = 128
HEADS = 3
TILES = 8
POOL = 16
SHARED = 4
KEYS = SHARED + POOL
SEQ = 64
PLANE = 8
ZS = 8
YS = 8
QB = 256
SPLITS = ((0, 96), (96, 32))
WINDOW = 12
MESH = pl.DeviceIdType.MESH
SCALE = HD**-0.5 * math.log2(math.e)
BIG = 1e30


def relatives():
    order = []
    for dx in (0, 1, 3, 2):
        for dc in range(2):
            for dz in (4, 3, 5, 2, 6, 1, 7, 0):
                if (dz, dx, dc) != (0, 0, 0):
                    order.append((dz, dx, dc))
    return order


def to_seq(place, copy_args):
    src, dst, send, recv = copy_args
    return pltpu.make_async_remote_copy(
        src, dst, send, recv, device_id={"seq": place}, device_id_type=MESH
    )


def kernel(
    code, holder, q_ref, k_ref, v_ref, bias_ref, out_ref,
    send_k, send_v0, send_v1, recv_k, recv_v0, recv_v1, shared, k_t, v_t,
    k_cat, v_cat, probs, scores, norm, y_send0, y_send1, y_recv0, y_recv1,
    k_send_sem, k_recv_sem, v_send_sem, v_recv_sem, r_send_sem, r_recv_sem,
    p_send_sem, p_recv_sem, y_send_sem, y_recv_sem,
):
    me = lax.axis_index("seq")
    my_y = lax.axis_index("head")
    z, piece = me // PLANE, me % PLANE
    x, core = piece // 2, piece % 2
    dist = jnp.minimum(z, ZS - z)

    barrier = pltpu.get_barrier_semaphore()

    @pl.loop(1, SEQ)
    def _(d):
        pl.semaphore_signal(
            barrier, inc=1, device_id={"seq": (me + d) % SEQ}, device_id_type=MESH
        )

    @pl.loop(1, YS)
    def _(d):
        pl.semaphore_signal(
            barrier, inc=1, device_id={"head": (my_y + d) % YS}, device_id_type=MESH
        )

    for h in range(HEADS):
        for s in range(TILES):
            k_t[h * TILES + s] = k_ref[s * TILE : (s + 1) * TILE, h * HD : (h + 1) * HD]

    @pl.loop(0, SEQ)
    def _(r):
        send_k[r] = k_t[code[r]]

    for h in range(HEADS):
        for s in range(TILES):
            v_t[h * TILES + s] = v_ref[s * TILE : (s + 1) * TILE, h * HD : (h + 1) * HD].T

    @pl.when(me == 0)
    def _():
        for j in range(SHARED):
            for h in range(HEADS):
                rows = slice(h * TILE, (h + 1) * TILE)
                shared[2 * j, rows] = k_ref[j * TILE : (j + 1) * TILE, h * HD : (h + 1) * HD]
                shared[2 * j + 1, rows] = v_t[h * TILES + j]

    recv_k[me] = send_k[me]

    pl.semaphore_wait(barrier, SEQ - 1 + YS - 1)

    def from_root(p):
        return to_seq(p, (shared.at[p], shared.at[p], p_send_sem.at[p], r_recv_sem))

    @pl.when(me == 0)
    def _():
        for p in range(1, PLANE):
            from_root(p).start()

    def along(step, slot):
        place = ((z + step) % ZS) * PLANE + piece
        return to_seq(
            place, (shared.at[piece], shared.at[piece], r_send_sem.at[slot], r_recv_sem)
        )

    def in_plane(q):
        return to_seq(
            z * PLANE + q,
            (shared.at[piece], shared.at[piece], p_send_sem.at[PLANE + q], p_recv_sem.at[piece]),
        )

    up = jnp.logical_and(z < 4, True)
    down = jnp.logical_or(z == 0, z > 5)

    def relay():
        @pl.when(me != 0)
        def _():
            along(1, 0).wait_recv()

        @pl.when(up)
        def _():
            along(1, 0).start()

        @pl.when(down)
        def _():
            along(ZS - 1, 1).start()

        @pl.loop(0, PLANE)
        def _(q):
            @pl.when(jnp.logical_and(q != piece, z * PLANE + q != 0))
            def _():
                in_plane(q).start()

    order = relatives()

    def place_of(rel):
        dz, dx, dc = rel
        return ((z + dz) % ZS) * PLANE + ((x + dx) % 4) * 2 + (core + dc) % 2

    def k_copy(rel, n):
        place = place_of(rel)
        return to_seq(
            place,
            (send_k.at[place], recv_k.at[me], k_send_sem.at[n % WINDOW], k_recv_sem.at[me]),
        )

    for n, rel in enumerate(order):
        if n >= WINDOW:
            k_copy(rel, n).wait_send()
        if n in (4, 16, 26, 36, 46):
            stage = (4, 16, 26, 36, 46).index(n)

            @pl.when(dist == stage)
            def _():
                relay()

        k_copy(rel, n).start()
        if n == 0:
            @pl.loop(0, SEQ)
            def _(r):
                tile = v_t[code[r]]
                send_v0[r] = tile[:96]
                send_v1[r] = tile[96:]

            recv_v0[me] = send_v0[me]
            recv_v1[me] = send_v1[me]

    def v_copy(part, place):
        src, dst = ((send_v0, recv_v0), (send_v1, recv_v1))[part]
        return to_seq(
            place,
            (src.at[place], dst.at[me], v_send_sem.at[part], v_recv_sem.at[part, me]),
        )

    for part in range(2):
        for rel in order:
            v_copy(part, place_of(rel)).start()

    @pl.when(me != 0)
    def _():
        @pl.loop(0, PLANE)
        def _(q):
            @pl.when(q != piece)
            def _():
                to_seq(
                    0, (shared.at[q], shared.at[q], p_send_sem.at[0], p_recv_sem.at[q])
                ).wait_recv()

    @pl.loop(0, SEQ)
    def _(r):
        @pl.when(r != me)
        def _():
            to_seq(
                0, (send_k.at[0], recv_k.at[r], k_send_sem.at[0], k_recv_sem.at[r])
            ).wait_recv()

    @pl.loop(0, HEADS)
    def _(h):
        for j in range(SHARED):
            k_cat[j * TILE : (j + 1) * TILE] = shared[
                2 * j, pl.ds(pl.multiple_of(h * TILE, TILE), TILE)
            ]
        for p in range(POOL):
            lo = (SHARED + p) * TILE
            k_cat[lo : lo + TILE] = recv_k[holder[h * POOL + p]]

        @pl.loop(0, TILES * TILE // QB)
        def _(b):
            q_at = pl.multiple_of(b * QB, QB)
            q_blk = q_ref[pl.ds(q_at, QB), pl.ds(pl.multiple_of(h * HD, HD), HD)]
            scores[...] = lax.dot_general(
                k_cat[...], q_blk, (((1,), (1,)), ((), ())), preferred_element_type=jnp.float32
            )
            bias = bias_ref[h, :, pl.ds(q_at, QB)]
            top = jnp.full((1, QB), -BIG, jnp.float32)
            for j in range(KEYS):
                tile_top = jnp.max(scores[j * TILE : (j + 1) * TILE], 0, keepdims=True)
                top = jnp.maximum(top, tile_top * SCALE - bias[j : j + 1])
            total = jnp.zeros((1, QB), jnp.float32)
            for j in range(KEYS):
                rows = slice(j * TILE, (j + 1) * TILE)
                weights = jnp.exp2(scores[rows] * SCALE - (top + bias[j : j + 1]))
                total = total + jnp.sum(weights, 0, keepdims=True)
                probs[h, rows, pl.ds(q_at, QB)] = weights.astype(jnp.bfloat16)
            norm[h, :, pl.ds(q_at, QB)] = 1.0 / total

    for part in range(2):
        src, recv = ((send_v0, recv_v0), (send_v1, recv_v1))[part]
        y_send, y_recv = ((y_send0, y_recv0), (y_send1, y_recv1))[part]
        d_at, d_size = SPLITS[part]

        @pl.loop(0, SEQ)
        def _(r):
            @pl.when(r != me)
            def _():
                to_seq(
                    0, (src.at[0], recv.at[r], v_send_sem.at[0], v_recv_sem.at[part, r])
                ).wait_recv()

        @pl.loop(0, HEADS)
        def _(h):
            for j in range(SHARED):
                v_cat[h, :d_size, j * TILE : (j + 1) * TILE] = shared[
                    2 * j + 1, pl.ds(pl.multiple_of(h * HD + d_at, 32), d_size)
                ]
            for p in range(POOL):
                lo = (SHARED + p) * TILE
                v_cat[h, :d_size, lo : lo + TILE] = recv[holder[h * POOL + p]]

        def y_copy(t):
            return pltpu.make_async_remote_copy(
                y_send.at[t],
                y_recv.at[my_y],
                y_send_sem.at[part],
                y_recv_sem.at[part, my_y],
                device_id={"head": t},
                device_id_type=MESH,
            )

        def send_pair(b):
            for i in range(QB // TILE):
                t = b * (QB // TILE) + i

                @pl.when(t != my_y)
                def _():
                    y_copy(t).start()

        blocks = TILES * TILE // QB

        def block_of(i):
            return (my_y // 2 + (2, 1, 3, 0)[i]) % blocks

        for i in range(blocks):
            b = block_of(i)
            q_at = pl.multiple_of(b * QB, QB)

            @pl.loop(0, HEADS)
            def _(h):
                o = jnp.dot(
                    v_cat[h, :d_size], probs[h, :, pl.ds(q_at, QB)],
                    preferred_element_type=jnp.float32,
                )
                o = (o * norm[h, :, pl.ds(q_at, QB)]).astype(jnp.bfloat16)
                for k in range(QB // TILE):
                    y_send[
                        b * (QB // TILE) + k, pl.ds(pl.multiple_of(h * d_size, 32), d_size)
                    ] = o[:, k * TILE : (k + 1) * TILE]

            if i > 0:
                send_pair(block_of(i - 1))
        y_recv[my_y] = y_send[my_y]
        send_pair(block_of(blocks - 1))

    for part in range(2):
        y_send, y_recv = ((y_send0, y_recv0), (y_send1, y_recv1))[part]

        @pl.loop(0, YS)
        def _(g):
            @pl.when(g != my_y)
            def _():
                pltpu.make_async_remote_copy(
                    y_send.at[0], y_recv.at[g], y_send_sem.at[part], y_recv_sem.at[part, g],
                    device_id={"head": 0}, device_id_type=MESH,
                ).wait_recv()

    for g in range(YS):
        for h in range(HEADS):
            both = jnp.concatenate(
                [y_recv0[g, h * 96 : (h + 1) * 96], y_recv1[g, h * 32 : (h + 1) * 32]], 0
            )
            lo = (g * HEADS + h) * HD
            out_ref[:, lo : lo + HD] = both.T

    for n in range(WINDOW):
        k_copy(order[0], n).wait_send()
    for part in range(2):
        @pl.loop(0, SEQ - 1)
        def _(r):
            v_copy(part, 0).wait_send()

        y_send, y_recv = ((y_send0, y_recv0), (y_send1, y_recv1))[part]

        @pl.loop(0, YS - 1)
        def _(r):
            pltpu.make_async_remote_copy(
                y_send.at[0], y_recv.at[0], y_send_sem.at[part], y_recv_sem.at[part, 0],
                device_id={"head": 0}, device_id_type=MESH,
            ).wait_send()

    @pl.when(me == 0)
    def _():
        for p in range(1, PLANE):
            from_root(p).wait_send()

    @pl.when(up)
    def _():
        along(1, 0).wait_send()

    @pl.when(down)
    def _():
        along(ZS - 1, 1).wait_send()

    @pl.loop(0, PLANE)
    def _(q):
        @pl.when(jnp.logical_and(q != piece, z * PLANE + q != 0))
        def _():
            in_plane(q).wait_send()


def body(queries, keys, values, tile_pool, tile_lists, key_slot):
    me = lax.axis_index("seq")
    slots = me * TILES + jnp.arange(TILES, dtype=jnp.int32)
    ids = jnp.arange(key_slot.shape[0], dtype=jnp.int32)
    stored = jnp.sum(jnp.where(key_slot[None] == slots[:, None], ids[None], 0), 1)
    wanted = (tile_pool.reshape(HEADS, SEQ, POOL)[..., None] == stored).astype(jnp.int32)
    codes = jnp.arange(HEADS * TILES, dtype=jnp.int32).reshape(HEADS, 1, 1, TILES)
    code = jnp.sum(wanted * codes, (0, 2, 3))
    own = lax.dynamic_slice_in_dim(tile_pool, me * POOL, POOL, 1).reshape(-1)
    holder = jnp.sum(jnp.where(own[:, None] == ids[None], key_slot[None] // TILES, 0), 1)
    listed = jnp.any(
        tile_lists[:, None] == jnp.arange(POOL, dtype=jnp.int32)[None, :, None, None], -1
    )
    bias = jnp.where(listed, 0.0, BIG).astype(jnp.float32)
    bias = jnp.concatenate([jnp.zeros((HEADS, SHARED, TILES), jnp.float32), bias], 1)
    bias = jnp.repeat(bias, TILE, 2)

    smem = pl.BlockSpec(memory_space=pltpu.SMEM)
    vmem = pl.BlockSpec(memory_space=pltpu.VMEM)
    bf16, f32 = jnp.bfloat16, jnp.float32
    dma = pltpu.SemaphoreType.DMA
    d0, d1 = SPLITS[0][1], SPLITS[1][1]
    return pl.pallas_call(
        kernel,
        out_shape=jax.ShapeDtypeStruct((TILE, YS * HEADS * HD), bf16),
        in_specs=[smem] * 2 + [vmem] * 4,
        out_specs=vmem,
        scratch_shapes=[
            pltpu.VMEM((SEQ, TILE, HD), bf16),
            pltpu.VMEM((SEQ, d0, TILE), bf16),
            pltpu.VMEM((SEQ, d1, TILE), bf16),
            pltpu.VMEM((SEQ, TILE, HD), bf16),
            pltpu.VMEM((SEQ, d0, TILE), bf16),
            pltpu.VMEM((SEQ, d1, TILE), bf16),
            pltpu.VMEM((PLANE, HEADS * TILE, TILE), bf16),
            pltpu.VMEM((HEADS * TILES, TILE, HD), bf16),
            pltpu.VMEM((HEADS * TILES, HD, TILE), bf16),
            pltpu.VMEM((KEYS * TILE, HD), bf16),
            pltpu.VMEM((HEADS, d0, KEYS * TILE), bf16),
            pltpu.VMEM((HEADS, KEYS * TILE, TILES * TILE), bf16),
            pltpu.VMEM((KEYS * TILE, QB), f32),
            pltpu.VMEM((HEADS, 1, TILES * TILE), f32),
            pltpu.VMEM((TILES, HEADS * d0, TILE), bf16),
            pltpu.VMEM((TILES, HEADS * d1, TILE), bf16),
            pltpu.VMEM((YS, HEADS * d0, TILE), bf16),
            pltpu.VMEM((YS, HEADS * d1, TILE), bf16),
            dma((WINDOW,)),
            dma((SEQ,)),
            dma((2,)),
            dma((2, SEQ)),
            dma((2,)),
            dma,
            dma((2 * PLANE,)),
            dma((PLANE,)),
            dma((2,)),
            dma((2, YS)),
        ],
        compiler_params=pltpu.CompilerParams(
            collective_id=0, has_side_effects=True, vmem_limit_bytes=60 * 2**20
        ),
        name="attend",
    )(code, holder, queries, keys, values, bias)


def solution(mesh):
    return jax.shard_map(
        body,
        mesh=mesh,
        in_specs=(
            P("seq", "head"),
            P("seq", "head"),
            P("seq", "head"),
            P("head", None),
            P("head", "seq", None),
            P(),
        ),
        out_specs=P(("seq", "head"), None),
        check_vma=False,
    )
```

time: 392 us -> 147 us (0.38)
  waiting for transfers between devices: 214 us -> 0 us
  Pallas kernels: 0 us -> 141 us
  local copies, waits for them, and re-layouts: 55.9 us -> 4.12 us
  matrix products: 26.3 us -> 0 us
  blocking collectives: 26.3 us -> 0 us
  starting transfers between devices: 21.7 us -> 0 us
  other arithmetic: 18.2 us -> 1.72 us
  between operations: 13.6 us -> 0.06 us
  loops' own time: 12.1 us -> 0 us
    pallas_call x0 -> x1, Pallas kernels: none -> 141 us  [body(): pl.pallas_call(kernel, out_shape=jax.ShapeDtypeStruct((TILE, YS * HEADS *...]
    psum x1 -> x0, waiting for transfers between devices: 116 us -> none  [from_root(): return lax.psum(kept, axis)]
    all_to_all x2 -> x0, waiting for transfers between devices: 98.1 us -> none  [the longest x1 94.4 us: body(): lax.all_to_all(flat_kv[incoming], 'seq', split_axis=0, concat_axis=0, til...]
    all_to_all x1 -> x0, blocking collectives: 26.3 us -> none  [body(): lax.all_to_all(result, 'head', split_axis=0, concat_axis=1, tiled=True)]
    dot_general x12 -> x0, matrix products: 26.3 us -> none  [the longest x6 13.4 us: finish(): jnp.einsum(pattern, weights.astype(jnp.bfloat16), value_part, preferred_e...]
    gather x10 -> x0, local copies, waits for them, and re-layouts: 23.5 us -> none  [the longest x6 15.1 us: per_block(): listed = pool_tiles[head_id][list_blk]]
    all_to_all x2 -> x0, starting transfers between devices: 21.7 us -> none  [the longest x1 14.8 us: body(): lax.all_to_all(outgoing, 'seq', split_axis=0, concat_axis=0, tiled=True)]
    another operation x1 -> x0, loops' own time: 12.1 us -> none  [body(): per_blocks = lax.map(per_block, (query_blocks, list_blocks, head_of))]
  transfers between devices with their start and end apart: 3 -> 0, of which waited for: 3 -> 0; matrix products, arithmetic and copies ran while one was open for 3% -> 0% of each run, Pallas kernels for 0% -> 0%
where the time goes in v1:
time: 147 us
  Pallas kernels  141 us (96%)
  local copies, waits for them, and re-layouts  4.12 us (3%)
  other arithmetic  1.72 us (1%)
    pallas_call x1, Pallas kernels, body(): pl.pallas_call(kernel, out_shape=jax.ShapeDtypeStruct((TILE, YS * HEADS *...  141 us

profile of v1, /device:TPU:1, one launch (start us, length us, event | category | flops | bytes accessed | tf_op | source)
XLA Modules:
  0.0 146.6 jit_solution(18140699776902323240)
XLA Ops:
  0.0 0.0 copy-start
  0.0 0.0 copy-start.2
  0.0 0.0 copy-start.1
  0.0 0.7 copy-done.2
  0.7 0.2 select_reduce_fusion.2
  0.9 0.0 copy-done
  0.9 0.1 constant_dynamic-slice_fusion
  1.0 0.1 eq.63
  1.1 0.7 select_reduce_fusion.1.holder
  1.7 0.0 copy-done.1
  1.7 0.1 copy.8
  1.8 0.1 fusion
  2.0 0.1 copy.10
  2.0 0.1 eq.56
  2.1 0.1 copy.7
  2.2 0.7 select_reduce_fusion.code
  2.9 0.1 broadcast_in_dim.50
  3.1 0.8 reshape.57.bias_ref
  3.8 140.7 %attend.1 = bf16[128,3072]{1,0:T(8,128)(2,1)} custom-call(s32[64]{0:T(128)} %select_reduce_fusion.code, s32[48]{0:T(128)} %select_reduce_fusion.1.holder, bf16[1024,384]{1,0:T(8,128)(2,1)} %q_ref.1, bf16[1024,384]{1,0:T(8,128)(2,1)} %k_ref.1, bf16[1024,384]{1,0:T(8,128)(2,1)} %v_ref.1, f32[3,20,1024]{2,1,0:T(8,128)} %reshape.57.bias_ref), custom_call_target="tpu_custom_call" | custom-call | tf_op jit(solution)/shard_map/attend/pallas_call | solution.py:378
  144.5 2.1 %copy.12 = bf16[128,3072]{1,0:T(8,128)(2,1)} copy(bf16[128,3072]{1,0:T(8,128)(2,1)} %attend.1) | data formatting | bytes 1572864
  (5 shorter events, 0.0 us)
Async XLA Ops:
  0.0 0.9 copy-start
  0.0 0.7 copy-start.2
  0.0 1.7 %copy-start.1 = (s32[3,8,12]{2,1,0:T(8,128)S(1)}, s32[3,8,12]{2,1,0:T(8,128)}, u32[]{:S(2)}) copy-start(s32[3,8,12]{2,1,0:T(8,128)} %param.10) | copy-start | bytes 3460

commit v2 on v1

v2 whole, which is shorter than its diff:
```python
import functools
import math

import jax
import jax.numpy as jnp
from jax import lax
from jax.experimental import pallas as pl
from jax.experimental.pallas import tpu as pltpu
from jax.sharding import PartitionSpec as P

TILE = 128
HD = 128
HEADS = 3
TILES = 8
POOL = 16
LIST = 12
SHARED = 4
KEYS = SHARED + POOL
SEQ = 64
PLANE = 8
ZS = 8
YS = 8
QB = 256
SPLITS = ((0, 64), (64, 32), (96, 32))
PARTS = len(SPLITS)
WINDOW = 12
STAGES = (24, 40, 56, 75, 97)
MESH = pl.DeviceIdType.MESH
SCALE = HD**-0.5 * math.log2(math.e)
BIG = 1e30


def relatives():
    order = []
    for dx in (0, 1, 3, 2):
        for dc in range(2):
            for dz in (4, 3, 5, 2, 6, 1, 7, 0):
                if (dz, dx, dc) != (0, 0, 0):
                    order.append((dz, dx, dc))
    return order


def to_seq(place, copy_args):
    src, dst, send, recv = copy_args
    return pltpu.make_async_remote_copy(
        src, dst, send, recv, device_id={"seq": place}, device_id_type=MESH
    )


def kernel(
    q_hbm, k_hbm, v_hbm, pool_hbm, lists_hbm, slot_hbm, *refs,
):
    y_recv, refs = refs[:PARTS], refs[PARTS:]
    v_send, refs = refs[:PARTS], refs[PARTS:]
    v_recv, refs = refs[:PARTS], refs[PARTS:]
    y_send, refs = refs[:PARTS], refs[PARTS:]
    (
        q_ref, k_ref, v_ref, pool_ref, lists_ref, slot_ref, pool_s, slot_s, table_v, table,
        k_send, k_recv, shared, k_t, v_t, bias_ref, k_cat, v_cat, probs, scores, norm,
        load_sem, table_sem, w_send_sem, k_recv_sem, v_send_sem, v_recv_sem,
        r_send_sem, r_recv_sem, p_send_sem, p_recv_sem, y_send_sem, y_recv_sem,
    ) = refs
    me = lax.axis_index("seq")
    my_y = lax.axis_index("head")
    z, piece = me // PLANE, me % PLANE
    x, core = piece // 2, piece % 2
    dist = jnp.minimum(z, ZS - z)

    loads = [
        pltpu.make_async_copy(src, dst, load_sem.at[n])
        for n, (src, dst) in enumerate(
            (
                (slot_hbm, slot_ref),
                (pool_hbm, pool_ref),
                (k_hbm, k_ref),
                (v_hbm, v_ref),
                (lists_hbm, lists_ref),
                (q_hbm, q_ref),
                (pool_hbm, pool_s),
                (slot_hbm, slot_s),
            )
        )
    ]
    for load in loads:
        load.start()

    barrier = pltpu.get_barrier_semaphore()

    @pl.loop(1, SEQ)
    def _(d):
        pl.semaphore_signal(
            barrier, inc=1, device_id={"seq": (me + d) % SEQ}, device_id_type=MESH
        )

    @pl.loop(1, YS)
    def _(d):
        pl.semaphore_signal(
            barrier, inc=1, device_id={"head": (my_y + d) % YS}, device_id_type=MESH
        )

    loads[0].wait()
    loads[1].wait()
    f32, bf16, i32 = jnp.float32, jnp.bfloat16, jnp.int32
    ntiles, entries = slot_ref.shape[1], SEQ * POOL
    mine = me * TILES + lax.broadcasted_iota(i32, (TILES, ntiles), 0)
    ids = lax.broadcasted_iota(i32, (TILES, ntiles), 1)
    stored = jnp.sum(jnp.where(slot_ref[...] == mine, ids, 0), 1, keepdims=True)
    wanted = jnp.zeros((TILES, entries), i32)
    local = lax.broadcasted_iota(i32, (TILES, entries), 0)
    for h in range(HEADS):
        wanted = wanted + jnp.where(pool_ref[h : h + 1, :] == stored, local + h * TILES, 0)
    wanted = jnp.sum(wanted, 0, keepdims=True)
    for shift in (1, 2, 4, 8):
        wanted = wanted + pltpu.roll(wanted, shift, 1)
    table_v[...] = jnp.clip(wanted, 0, HEADS * TILES - 1)
    to_table = pltpu.make_async_copy(table_v, table, table_sem)
    to_table.start()

    def code(r):
        return jnp.clip(table[0, r * POOL + POOL - 1], 0, HEADS * TILES - 1)

    def holder(h, p):
        tile = jnp.clip(pool_s[h, me * POOL + p], 0, ntiles - 1)
        return jnp.clip(slot_s[0, tile] // TILES, 0, SEQ - 1)

    loads[2].wait()
    for h in range(HEADS):
        for s in range(TILES):
            k_t[h * TILES + s] = k_ref[s * TILE : (s + 1) * TILE, h * HD : (h + 1) * HD]
    to_table.wait()

    @pl.loop(0, SEQ)
    def _(r):
        k_send[r] = k_t[code(r)]

    @pl.when(me == 0)
    def _():
        for j in range(SHARED):
            for h in range(HEADS):
                shared[2 * j, h * TILE : (h + 1) * TILE] = k_t[h * TILES + j]

    k_recv[me] = k_send[me]

    pl.semaphore_wait(barrier, SEQ - 1 + YS - 1)

    def from_root(p):
        return to_seq(p, (shared.at[p], shared.at[p], p_send_sem.at[p], r_recv_sem))

    @pl.when(me == 0)
    def _():
        for p in range(2, PLANE, 2):
            from_root(p).start()

    def along(step, slot):
        place = ((z + step) % ZS) * PLANE + piece
        return to_seq(
            place, (shared.at[piece], shared.at[piece], r_send_sem.at[slot], r_recv_sem)
        )

    def in_plane(q):
        return to_seq(
            z * PLANE + q,
            (shared.at[piece], shared.at[piece], p_send_sem.at[PLANE + q], p_recv_sem.at[piece]),
        )

    up = z < 4
    down = jnp.logical_or(z == 0, z > 5)

    def relay():
        @pl.when(me != 0)
        def _():
            along(1, 0).wait_recv()

        @pl.when(up)
        def _():
            along(1, 0).start()

        @pl.when(down)
        def _():
            along(ZS - 1, 1).start()

        @pl.loop(0, PLANE)
        def _(q):
            @pl.when(jnp.logical_and(q != piece, z * PLANE + q != 0))
            def _():
                in_plane(q).start()

    def pack_values():
        loads[3].wait()
        for h in range(HEADS):
            for s in range(TILES):
                v_t[h * TILES + s] = flip(
                    v_ref[s * TILE : (s + 1) * TILE, h * HD : (h + 1) * HD]
                )

        @pl.when(me == 0)
        def _():
            for j in range(SHARED):
                for h in range(HEADS):
                    shared[2 * j + 1, h * TILE : (h + 1) * TILE] = v_t[h * TILES + j]

        @pl.loop(0, SEQ)
        def _(r):
            tile = v_t[code(r)]
            for (d_at, d_size), send in zip(SPLITS, v_send):
                send[r] = tile[d_at : d_at + d_size]

        for send, recv in zip(v_send, v_recv):
            recv[me] = send[me]

        @pl.when(me == 0)
        def _():
            for p in range(1, PLANE, 2):
                from_root(p).start()

    def make_bias():
        loads[4].wait()
        pool_ids = lax.broadcasted_iota(i32, (TILES, POOL), 1)
        spread = (
            lax.broadcasted_iota(i32, (TILES, TILES * TILE), 1) // TILE
            == lax.broadcasted_iota(i32, (TILES, TILES * TILE), 0)
        ).astype(bf16)
        for h in range(HEADS):
            listed = jnp.zeros((TILES, POOL), f32)
            for l in range(LIST):
                listed = jnp.where(lists_ref[h, :, l : l + 1] == pool_ids, 1.0, listed)
            rows = lax.dot_general(
                listed.astype(bf16), spread, (((0,), (0,)), ((), ())), preferred_element_type=f32
            )
            bias_ref[h] = jnp.where(rows > 0.5, 0.0, BIG)

    order = relatives()

    def place_of(rel):
        dz, dx, dc = rel
        return ((z + dz) % ZS) * PLANE + ((x + dx) % 4) * 2 + (core + dc) % 2

    def k_copy(rel, n):
        place = place_of(rel)
        sem = w_send_sem.at[n % WINDOW]
        return to_seq(place, (k_send.at[place], k_recv.at[me], sem, k_recv_sem.at[me]))

    def v_copy(part, place, sem):
        return to_seq(
            place,
            (v_send[part].at[place], v_recv[part].at[me], sem, v_recv_sem.at[part, me]),
        )

    def windowed(n):
        if n < SEQ - 1:
            return k_copy(order[n], n)
        rel = order[n - SEQ + 1]
        return v_copy(0, place_of(rel), w_send_sem.at[n % WINDOW])

    count = STAGES[-1] + 1
    for n in range(count):
        if n == WINDOW:
            pack_values()
            make_bias()
        if n >= WINDOW:
            windowed(n - WINDOW).wait_send()
        if n in STAGES:

            @pl.when(dist == STAGES.index(n))
            def _():
                relay()

        windowed(n).start()
    for n in range(count, 2 * (SEQ - 1)):
        v_copy(0, place_of(order[n - SEQ + 1]), v_send_sem.at[0]).start()
    for part in range(1, PARTS):
        for rel in order:
            v_copy(part, place_of(rel), v_send_sem.at[part]).start()

    @pl.when(me != 0)
    def _():
        @pl.loop(0, PLANE)
        def _(q):
            @pl.when(q != piece)
            def _():
                to_seq(
                    0, (shared.at[q], shared.at[q], p_send_sem.at[0], p_recv_sem.at[q])
                ).wait_recv()

    loads[6].wait()
    loads[7].wait()

    @pl.loop(0, SEQ)
    def _(r):
        @pl.when(r != me)
        def _():
            to_seq(
                0, (k_send.at[0], k_recv.at[r], w_send_sem.at[0], k_recv_sem.at[r])
            ).wait_recv()

    loads[5].wait()

    @pl.loop(0, HEADS)
    def _(h):
        for j in range(SHARED):
            k_cat[j * TILE : (j + 1) * TILE] = shared[
                2 * j, pl.ds(pl.multiple_of(h * TILE, TILE), TILE)
            ]
        for p in range(POOL):
            lo = (SHARED + p) * TILE
            k_cat[lo : lo + TILE] = k_recv[holder(h, p)]

        @pl.loop(0, TILES * TILE // QB)
        def _(b):
            q_at = pl.multiple_of(b * QB, QB)
            q_blk = q_ref[pl.ds(q_at, QB), pl.ds(pl.multiple_of(h * HD, HD), HD)]
            scores[...] = lax.dot_general(
                k_cat[...], q_blk, (((1,), (1,)), ((), ())), preferred_element_type=f32
            )
            bias = bias_ref[h, :, pl.ds(q_at, QB)]
            top = jnp.full((1, QB), -BIG, f32)
            for j in range(KEYS):
                tile_top = jnp.max(scores[j * TILE : (j + 1) * TILE], 0, keepdims=True) * SCALE
                if j >= SHARED:
                    tile_top = tile_top - bias[j - SHARED : j - SHARED + 1]
                top = jnp.maximum(top, tile_top)
            total = jnp.zeros((1, QB), f32)
            for j in range(KEYS):
                rows = slice(j * TILE, (j + 1) * TILE)
                less = top
                if j >= SHARED:
                    less = top + bias[j - SHARED : j - SHARED + 1]
                weights = jnp.exp2(scores[rows] * SCALE - less)
                total = total + jnp.sum(weights, 0, keepdims=True)
                probs[h, rows, pl.ds(q_at, QB)] = weights.astype(bf16)
            norm[h, :, pl.ds(q_at, QB)] = 1.0 / total

    for part in range(PARTS):
        d_at, d_size = SPLITS[part]

        @pl.loop(0, SEQ)
        def _(r):
            @pl.when(r != me)
            def _():
                to_seq(
                    0,
                    (
                        v_send[part].at[0],
                        v_recv[part].at[r],
                        v_send_sem.at[0],
                        v_recv_sem.at[part, r],
                    ),
                ).wait_recv()

        @pl.loop(0, HEADS)
        def _(h):
            for j in range(SHARED):
                v_cat[h, :d_size, j * TILE : (j + 1) * TILE] = shared[
                    2 * j + 1, pl.ds(pl.multiple_of(h * HD + d_at, 32), d_size)
                ]
            for p in range(POOL):
                lo = (SHARED + p) * TILE
                v_cat[h, :d_size, lo : lo + TILE] = v_recv[part][holder(h, p)]

        def y_copy(t):
            return pltpu.make_async_remote_copy(
                y_send[part].at[t],
                y_recv[part].at[my_y],
                y_send_sem.at[part],
                y_recv_sem.at[part, my_y],
                device_id={"head": t},
                device_id_type=MESH,
            )

        def send_pair(b):
            for i in range(QB // TILE):
                t = b * (QB // TILE) + i

                @pl.when(t != my_y)
                def _():
                    y_copy(t).start()

        blocks = TILES * TILE // QB

        def block_of(i):
            return (my_y // 2 + (2, 1, 3, 0)[i]) % blocks

        for i in range(blocks):
            b = block_of(i)
            q_at = pl.multiple_of(b * QB, QB)

            @pl.loop(0, HEADS)
            def _(h):
                o = jnp.dot(
                    v_cat[h, :d_size], probs[h, :, pl.ds(q_at, QB)], preferred_element_type=f32
                )
                o = (o * norm[h, :, pl.ds(q_at, QB)]).astype(bf16)
                for k in range(QB // TILE):
                    y_send[part][
                        b * (QB // TILE) + k, pl.ds(pl.multiple_of(h * d_size, 32), d_size)
                    ] = o[:, k * TILE : (k + 1) * TILE]

            if i > 0:
                send_pair(block_of(i - 1))
        y_recv[part][my_y] = y_send[part][my_y]
        send_pair(block_of(blocks - 1))

    def y_any(part, g):
        return pltpu.make_async_remote_copy(
            y_send[part].at[0], y_recv[part].at[g], y_send_sem.at[part], y_recv_sem.at[part, g],
            device_id={"head": 0}, device_id_type=MESH,
        )

    for n in range(count - WINDOW, count):
        windowed(n).wait_send()

    @pl.loop(0, 2 * (SEQ - 1) - count)
    def _(r):
        v_copy(0, 0, v_send_sem.at[0]).wait_send()

    for part in range(1, PARTS):

        @pl.loop(0, SEQ - 1)
        def _(r):
            v_copy(part, 0, v_send_sem.at[part]).wait_send()

    @pl.when(me == 0)
    def _():
        for p in range(1, PLANE):
            from_root(p).wait_send()

    @pl.when(up)
    def _():
        along(1, 0).wait_send()

    @pl.when(down)
    def _():
        along(ZS - 1, 1).wait_send()

    @pl.loop(0, PLANE)
    def _(q):
        @pl.when(jnp.logical_and(q != piece, z * PLANE + q != 0))
        def _():
            in_plane(q).wait_send()

    for part in range(PARTS):

        @pl.loop(0, YS)
        def _(g):
            @pl.when(g != my_y)
            def _():
                y_any(part, g).wait_recv()

        @pl.loop(0, YS - 1)
        def _(r):
            y_any(part, 0).wait_send()


def identity():
    rows = lax.broadcasted_iota(jnp.int32, (TILE, TILE), 0)
    return (rows == lax.broadcasted_iota(jnp.int32, (TILE, TILE), 1)).astype(jnp.bfloat16)


def flip(matrix):
    return lax.dot_general(
        identity(), matrix, (((1,), (1,)), ((), ())), preferred_element_type=jnp.float32
    ).astype(jnp.bfloat16)


def arrange(*refs):
    out_ref = refs[-1]
    for g in range(YS):
        for h in range(HEADS):
            rows = [
                ref[g, h * d_size : (h + 1) * d_size] for ref, (_, d_size) in zip(refs, SPLITS)
            ]
            lo = (g * HEADS + h) * HD
            out_ref[:, lo : lo + HD] = flip(jnp.concatenate(rows, 0))


def body(queries, keys, values, tile_pool, tile_lists, key_slot):
    anywhere = pl.BlockSpec(memory_space=pl.ANY)
    vmem = pl.BlockSpec(memory_space=pltpu.VMEM)
    bf16, f32, i32 = jnp.bfloat16, jnp.float32, jnp.int32
    dma = pltpu.SemaphoreType.DMA
    sizes = [d_size for _, d_size in SPLITS]
    v_bufs = [pltpu.VMEM((SEQ, d, TILE), bf16) for d in sizes]
    y_bufs = [pltpu.VMEM((TILES, HEADS * d, TILE), bf16) for d in sizes]
    key_slot = key_slot.reshape(1, -1)
    received = pl.pallas_call(
        kernel,
        out_shape=[jax.ShapeDtypeStruct((YS, HEADS * d, TILE), bf16) for d in sizes],
        in_specs=[anywhere] * 6,
        out_specs=[vmem] * PARTS,
        scratch_shapes=v_bufs
        + v_bufs
        + y_bufs
        + [
            pltpu.VMEM(queries.shape, bf16),
            pltpu.VMEM(keys.shape, bf16),
            pltpu.VMEM(values.shape, bf16),
            pltpu.VMEM(tile_pool.shape, i32),
            pltpu.VMEM(tile_lists.shape, i32),
            pltpu.VMEM(key_slot.shape, i32),
            pltpu.SMEM(tile_pool.shape, i32),
            pltpu.SMEM(key_slot.shape, i32),
            pltpu.VMEM((1, SEQ * POOL), i32),
            pltpu.SMEM((1, SEQ * POOL), i32),
            pltpu.VMEM((SEQ, TILE, HD), bf16),
            pltpu.VMEM((SEQ, TILE, HD), bf16),
            pltpu.VMEM((PLANE, HEADS * TILE, TILE), bf16),
            pltpu.VMEM((HEADS * TILES, TILE, HD), bf16),
            pltpu.VMEM((HEADS * TILES, HD, TILE), bf16),
            pltpu.VMEM((HEADS, POOL, TILES * TILE), f32),
            pltpu.VMEM((KEYS * TILE, HD), bf16),
            pltpu.VMEM((HEADS, max(sizes), KEYS * TILE), bf16),
            pltpu.VMEM((HEADS, KEYS * TILE, TILES * TILE), bf16),
            pltpu.VMEM((KEYS * TILE, QB), f32),
            pltpu.VMEM((HEADS, 1, TILES * TILE), f32),
            dma((8,)),
            dma,
            dma((WINDOW,)),
            dma((SEQ,)),
            dma((PARTS,)),
            dma((PARTS, SEQ)),
            dma((2,)),
            dma,
            dma((2 * PLANE,)),
            dma((PLANE,)),
            dma((PARTS,)),
            dma((PARTS, YS)),
        ],
        compiler_params=pltpu.CompilerParams(
            collective_id=0, has_side_effects=True, vmem_limit_bytes=56 * 2**20
        ),
        name="attend",
    )(queries, keys, values, tile_pool, tile_lists, key_slot)
    return pl.pallas_call(
        arrange,
        out_shape=jax.ShapeDtypeStruct((TILE, YS * HEADS * HD), bf16),
        in_specs=[vmem] * PARTS,
        out_specs=vmem,
        name="arrange",
    )(*received)


def solution(mesh):
    return jax.shard_map(
        body,
        mesh=mesh,
        in_specs=(
            P("seq", "head"),
            P("seq", "head"),
            P("seq", "head"),
            P("head", None),
            P("head", "seq", None),
            P(),
        ),
        out_specs=P(("seq", "head"), None),
        check_vma=False,
    )
```

time: 147 us -> 131 us (0.89)
  Pallas kernels: 141 us -> 130 us
  local copies, waits for them, and re-layouts: 4.12 us -> 0 us
  other arithmetic: 1.72 us -> 0 us
    pallas_call x1 -> x2, Pallas kernels: 141 us -> 130 us  [the longest x1 128 us: body(): pl.pallas_call(kernel, out_shape=[jax.ShapeDtypeStruct((YS, HEADS * d, TI...]
    unnamed x9 -> x0, local copies, waits for them, and re-layouts: 2.91 us -> none
    reduce_sum x3 -> x0, other arithmetic: 1.59 us -> none  [the longest x1 0.73 us: body(): code = jnp.sum(wanted * codes, (0, 2, 3))]
where the time goes in v2:
time: 131 us; the launch traced here: 130 us
  Pallas kernels  130 us (99%)
    pallas_call x1, Pallas kernels, body(): pl.pallas_call(kernel, out_shape=[jax.ShapeDtypeStruct((YS, HEADS * d, TI...  128 us
    pallas_call x1, Pallas kernels, body(): pl.pallas_call(arrange, out_shape=jax.ShapeDtypeStruct((TILE, YS * HEADS...  2.7 us

profile of v2, /device:TPU:1, one launch (start us, length us, event | category | flops | bytes accessed | tf_op | source)
XLA Modules:
  0.0 130.4 jit_solution(7292715593669456645)
XLA Ops:
  0.0 127.7 %attend.1 = (bf16[8,192,128]{2,1,0:T(8,128)(2,1)}, bf16[8,96,128]{2,1,0:T(8,128)(2,1)}, bf16[8,96,128]{2,1,0:T(8,128)(2,1)}) custom-call(bf16[1024,384]{1,0:T(8,128)(2,1)} %q_hbm.1, bf16[1024,384]{1,0:T(8,128)(2,1)} %k_hbm.1, bf16[1024,384]{1,0:T(8,128)(2,1)} %v_hbm.1, s32[3,1024]{1,0:T(4,128)} %pool_hbm.1, s32[3,8,12]{2,1,0:T(8,128)} %lists_hbm.1, ...), custom_call_target="tpu_custom_call" | custom-call | tf_op jit(solution)/shard_map/attend/pallas_call | solution.py:485
  127.7 2.7 %arrange.1 = bf16[128,3072]{1,0:T(8,128)(2,1)} custom-call(bf16[8,192,128]{2,1,0:T(8,128)(2,1)} %get-tuple-element.8.refs_0_, bf16[8,96,128]{2,1,0:T(8,128)(2,1)} %get-tuple-element.9.refs_1_, bf16[8,96,128]{2,1,0:T(8,128)(2,1)} %get-tuple-element.10.refs_2_), custom_call_target="tpu_custom_call" | custom-call | tf_op jit(solution)/shard_map/arrange/pallas_call | solution.py:533
